TPU v7x, 256 devices: a whole 4x4x8 slice. The times are simulated.
256 devices in a mesh: dp: 8 (over z), expert: 32 (over x, y, core).
Axes of the slice: x: 4, y: 4, z: 8, core: 2. Of those that a mesh axis runs over, the one named last changes fastest.
Arguments:
- tokens: bfloat16 [256, 212, 1024], P(('dp', 'expert')), may hold values from -6 to 6
- expert_ids: int32 [256, 212, 1], P(('dp', 'expert')), may hold values from 0 to 31; in each aligned block of 212 rows (0 to 211, 212 to 423, ..., all dimensions but the last counted through in order) at most 9 rows name the same one
- caption_lengths: int32 [256], P(('dp', 'expert')), may hold values from 1 to 16, as said below
- layer_norm_gain: float32 [1024], replicated, may hold values from 0.5 to 1.5
- router: float32 [1024, 32], replicated, may hold values from -0.1875 to 0.1875
- w_up: bfloat16 [32, 1024, 4096], P('expert', None, 'dp'), may hold values from -0.1875 to 0.1875
- w_down: bfloat16 [32, 4096, 1024], P('expert', 'dp'), may hold values from -0.09375 to 0.09375
- logit_scale: float32 [1], replicated, may hold values from 5 to 20
- logit_bias: float32 [1], replicated, may hold values from -4 to -1.5
Outputs:
- loss: float32 [1], replicated
- grad_tokens: bfloat16 [256, 212, 1024], P(('dp', 'expert'))
- grad_up: float32 [32, 1024, 4096], P('expert', None, 'dp')
- grad_down: float32 [32, 4096, 1024], P('expert', 'dp')
- grad_router: float32 [1024, 32], replicated
- layer_gain_gradient: float32 [1024], replicated
Inputs may be any that keep to these rules, and one draw needn't show every extreme that they name: `expert_ids`: among the rows of one device (aligned blocks of 212 rows, devices ordered by dp then expert) no expert is named more than 9 times, a bound that some block reaches. `caption_lengths`: some caption has all 16 tokens.
All inputs are finite; a program needn't handle non-finite values.
Results may differ from a plain program's by a relative error of at most 0.009.
Values may be sent and summed in bfloat16 or wider, within the bound.
No kernel may reach another device: no remote copies, remote signals or barrier semaphores. Data moves between devices by JAX's collectives and lax.ppermute only.
A program may use at most 128 MiB of HBM per device.

v0:
```python
import jax
import jax.numpy as jnp
from jax import lax
from jax.sharding import PartitionSpec as P

D = 1024
PATCH = 196
CAPLEN = 16
SEQ = 212
eps = 1e-06
loss_scale = 1024.0


def gelu_slope(pre):
    return (
        0.5 * (1.0 + lax.erf(pre * 0.7071067811865476))
        + pre * jnp.exp(-0.5 * pre * pre) * 0.3989422804014327
    )


def deliver(buffer, experts, slots):
    width = buffer.shape[-1]
    sent = lax.all_to_all(
        buffer.reshape(experts, 1, slots, width), "expert", split_axis=0, concat_axis=1, tiled=True
    )
    shaped = sent.reshape(sent.shape[0], 1, sent.shape[1], slots, width)
    whole = lax.all_gather(shaped, "dp", axis=1, tiled=True)
    return whole.reshape(whole.shape[0], -1, width)


def give_back(partial_value, n_dp, n_expert, slots):
    local = partial_value.shape[0]
    width = partial_value.shape[-1]
    summed = lax.psum_scatter(
        partial_value.reshape(local, n_dp, n_expert * slots, width).astype(jnp.bfloat16),
        "dp",
        scatter_dimension=1,
        tiled=True,
    )
    rounded = summed.reshape(local, n_expert, slots, width)
    returned = lax.all_to_all(rounded, "expert", split_axis=1, concat_axis=0, tiled=True)
    return returned.reshape(-1, width)


def body(
    tokens,
    expert_ids,
    caption_lengths,
    layer_norm_gain,
    router,
    w_up,
    w_down,
    logit_scale,
    logit_bias,
):
    n_dp = lax.axis_size("dp")
    n_expert = lax.axis_size("expert")
    pair_dev = tokens.shape[0]
    rows = pair_dev * SEQ
    experts = router.shape[1]
    slots = rows * 4 // (3 * experts) + 1
    pairs_all = pair_dev * n_dp * n_expert
    input_rows = tokens.reshape(rows, D).astype(jnp.float32)
    input_mean = jnp.mean(input_rows, axis=1, keepdims=True)
    var_x = jnp.mean((input_rows - input_mean) ** 2, axis=1, keepdims=True)
    inverse_deviation = 1.0 / jnp.sqrt(var_x + eps)
    centered_scaled_input = (input_rows - input_mean) * inverse_deviation
    normalized_input = (centered_scaled_input * layer_norm_gain).astype(jnp.bfloat16)
    ids = expert_ids.reshape(rows)
    onehot = (ids[:, None] == jnp.arange(experts, dtype=jnp.int32)[None, :]).astype(jnp.int32)
    slot = jnp.sum((jnp.cumsum(onehot, axis=0) - 1) * onehot, axis=1)
    dest = ids * slots + slot
    onehot_f = onehot.astype(jnp.float32)
    buffer = jnp.zeros((experts * slots, D), jnp.bfloat16).at[dest].set(normalized_input)
    gathered = deliver(buffer, experts, slots)
    pre = jnp.einsum("erd,edf->erf", gathered, w_up, preferred_element_type=jnp.float32)
    act = jax.nn.gelu(pre, approximate=False).astype(jnp.bfloat16)
    partial_value = jnp.einsum("erf,efd->erd", act, w_down, preferred_element_type=jnp.float32)
    moe = give_back(partial_value, n_dp, n_expert, slots)[dest].astype(jnp.float32)
    xnf = normalized_input.astype(jnp.float32)
    router_logits = jnp.dot(xnf, router, precision=lax.Precision.HIGHEST)
    gate = jax.nn.sigmoid(jnp.sum(router_logits * onehot_f, axis=1))
    y = (input_rows + gate[:, None] * moe).reshape(pair_dev, SEQ, D)
    img = jnp.mean(y[:, :PATCH], axis=1)
    lengths = caption_lengths.astype(jnp.float32)
    mask = (jnp.arange(CAPLEN, dtype=jnp.int32)[None, :] < caption_lengths[:, None]).astype(
        jnp.float32
    )
    txt = jnp.sum(y[:, PATCH:] * mask[:, :, None], axis=1) / lengths[:, None]
    ru = jnp.sqrt(jnp.mean(img * img, axis=1, keepdims=True) + eps)
    rv = jnp.sqrt(jnp.mean(txt * txt, axis=1, keepdims=True) + eps)
    u = img / ru
    v = txt / rv
    scale = logit_scale[0]
    first = lax.axis_index(("dp", "expert")) * pair_dev
    mine = first + jnp.arange(pair_dev, dtype=jnp.int32)
    every = jnp.arange(pairs_all, dtype=jnp.int32)
    own_sign = jnp.where(mine[:, None] == every[None, :], 1.0, -1.0)
    v_all = lax.all_gather(v, ("dp", "expert"), axis=0, tiled=True)
    logits = scale * jnp.dot(u, v_all.T, precision=lax.Precision.HIGHEST) / D + logit_bias[0]
    loss_term = -jnp.sum(jax.nn.log_sigmoid(own_sign * logits)) / pairs_all
    coef = -(loss_scale / pairs_all) * own_sign * jax.nn.sigmoid(-own_sign * logits)
    du = scale / D * jnp.dot(coef, v_all, precision=lax.Precision.HIGHEST)
    dv_terms = scale / D * jnp.dot(coef.T, u, precision=lax.Precision.HIGHEST)
    dv = lax.psum_scatter(dv_terms, ("dp", "expert"), scatter_dimension=0, tiled=True)
    dimg = (du - u * jnp.mean(du * u, axis=1, keepdims=True)) / ru
    dtxt = (dv - v * jnp.mean(dv * v, axis=1, keepdims=True)) / rv
    dy_img = jnp.broadcast_to(dimg[:, None, :] / PATCH, (pair_dev, PATCH, D))
    dy_txt = (dtxt / lengths[:, None])[:, None, :] * mask[:, :, None]
    dy = jnp.concatenate([dy_img, dy_txt], axis=1).reshape(rows, D)
    dmoe = (gate[:, None] * dy).astype(jnp.bfloat16)
    dgl = jnp.sum(dy * moe, axis=1) * gate * (1.0 - gate)
    router_part = jnp.dot(xnf.T, onehot_f * dgl[:, None], precision=lax.Precision.HIGHEST)
    grad_buffer = jnp.zeros((experts * slots, D), jnp.bfloat16).at[dest].set(dmoe)
    gathered_grads = deliver(grad_buffer, experts, slots)
    dact = jnp.einsum("erd,efd->erf", gathered_grads, w_down, preferred_element_type=jnp.float32)
    dpre = (dact * gelu_slope(pre)).astype(jnp.bfloat16)
    grad_down = jnp.einsum("erf,erd->efd", act, gathered_grads, preferred_element_type=jnp.float32)
    grad_up = jnp.einsum("erd,erf->edf", gathered, dpre, preferred_element_type=jnp.float32)
    back_partial = jnp.einsum("erf,edf->erd", dpre, w_up, preferred_element_type=jnp.float32)
    dxe = give_back(back_partial, n_dp, n_expert, slots)[dest].astype(jnp.float32)
    router_rows = jnp.dot(onehot_f, router.T, precision=lax.Precision.HIGHEST)
    gradient_normalized_input = dxe + dgl[:, None] * router_rows
    gain_partial_term = jnp.sum(gradient_normalized_input * centered_scaled_input, axis=0)
    scaled_output_gradient = gradient_normalized_input * layer_norm_gain
    normed_input_gradient = (
        scaled_output_gradient
        - jnp.mean(scaled_output_gradient, axis=1, keepdims=True)
        - centered_scaled_input
        * jnp.mean(scaled_output_gradient * centered_scaled_input, axis=1, keepdims=True)
    ) * inverse_deviation
    grad_tokens = (dy + normed_input_gradient).astype(jnp.bfloat16).reshape(pair_dev, SEQ, D)
    loss, grad_router, layer_gain_gradient = lax.psum(
        (loss_term, router_part, gain_partial_term), ("dp", "expert")
    )
    return (loss.reshape(1), grad_tokens, grad_up, grad_down, grad_router, layer_gain_gradient)


def solution(mesh):
    return jax.shard_map(
        body,
        mesh=mesh,
        in_specs=(
            P(("dp", "expert"), None, None),
            P(("dp", "expert"), None, None),
            P(("dp", "expert")),
            P(),
            P(),
            P("expert", None, "dp"),
            P("expert", "dp", None),
            P(),
            P(),
        ),
        out_specs=(
            P(),
            P(("dp", "expert"), None, None),
            P("expert", None, "dp"),
            P("expert", "dp", None),
            P(),
            P(),
        ),
        check_vma=False,
    )
```

profile of v0, /device:TPU:8, one launch (start us, length us, event | category | flops | bytes accessed | tf_op | source)
XLA Modules:
  0.0 1022.8 jit_solution(2046483523152713916)
XLA Ops:
  12.8 2.3 scatter_custom_fusion
  15.4 22.9 %all_to_all.16 = bf16[32,1,9,1024]{3,2,1,0:T(8,128)(2,1)S(1)} all-to-all(bf16[32,1,9,1024]{3,2,1,0:T(8,128)(2,1)S(1)} %bitcast.149), channel_id=1, replica_groups=mesh['dp'=8,'expert'=32] {'expert'}, dimensions={0} | all-to-all | bytes 1179648 | tf_op jit(solution)/shard_map/all_to_all | solution.py:23
  39.7 60.3 %all-gather.7.cloned.1.call-done = bf16[256,1,9,1024]{3,0,2,1:T(8,128)(2,1)} async-done(((bf16[32,1,9,1024]{3,0,2,1:T(8,128)(2,1)}), bf16[256,1,9,1024]{3,0,2,1:T(8,128)(2,1)}) %all-gather.7.cloned.1.call-update) | async-done | bytes 4718608 | tf_op jit(solution)/shard_map/all_gather | solution.py:27
  100.0 8.7 copy.22
  108.7 9.8 reshape.491
  118.6 14.9 %fusion.2 = (bf16[2304,512]{1,0:T(8,128)(2,1)S(1)}, f32[2304,512]{1,0:T(8,128)}) fusion(bf16[2304,1024]{1,0:T(8,128)(2,1)} %reshape.491, bf16[1,1024,512]{2,1,0:T(8,128)(2,1)S(1)} %copy-done), kind=kOutput, calls=%fused_computation.9 | convolution fusion | flops 2492596224 | bytes 12845056 | tf_op jit(solution)/shard_map/erd,edf->erf/dot_general | solution.py:76
  134.8 4.2 convert_bitcast_fusion.1
  139.8 58.3 %reduce-scatter.3.cloned.1.call-done = bf16[1,1,288,1024]{3,2,1,0:T(8,128)(2,1)} async-done(((bf16[1,8,288,1024]{3,2,1,0:T(8,128)(2,1)}), bf16[1,1,288,1024]{3,2,1,0:T(8,128)(2,1)}) %reduce-scatter.3.cloned.1.call-update) | async-done | bytes 589840 | tf_op jit(solution)/shard_map/reduce_scatter | solution.py:34
  198.1 2.2 reshape.494
  200.2 7.4 all-to-all-start.1
  208.8 14.4 %all-to-all-done.1 = bf16[1,32,9,1024]{3,2,0,1:T(8,128)(2,1)S(1)} async-done(((bf16[1,32,9,1024]{3,2,0,1:T(8,128)(2,1)}), bf16[1,32,9,1024]{3,2,0,1:T(8,128)(2,1)S(1)}, u32[]{:S(2)}, u32[]{:S(2)}) %all-to-all-start.1) | async-done | bytes 589856 | tf_op jit(solution)/shard_map/all_to_all | solution.py:41
  229.8 95.7 %all-gather.9.cloned.1.call-done = f32[262144]{0:T(1024)} async-done(((f32[1024]{0:T(1024)}), f32[262144]{0:T(1024)}) %all-gather.9.cloned.1.call-update) | async-done | bytes 1048592 | tf_op jit(solution)/shard_map/all_gather | solution.py:99
  331.5 254.7 %all-reduce.8.cloned.1.call-done = f32[256,1024]{1,0:T(8,128)} async-done(((f32[256,1024]{1,0:T(8,128)}), f32[256,1024]{1,0:T(8,128)}) %all-reduce.8.cloned.1.call-update) | async-done | bytes 1048592
  589.2 2.5 scatter_custom_fusion.1
  593.0 22.3 %all_to_all.17 = bf16[32,1,9,1024]{3,2,1,0:T(8,128)(2,1)S(1)} all-to-all(bf16[32,1,9,1024]{3,2,1,0:T(8,128)(2,1)S(1)} %bitcast.150), channel_id=1, replica_groups=mesh['dp'=8,'expert'=32] {'expert'}, dimensions={0} | all-to-all | bytes 1179648 | tf_op jit(solution)/shard_map/all_to_all | solution.py:23
  616.6 57.0 %all-gather.11.cloned.1.call-done = bf16[256,1,9,1024]{3,0,2,1:T(8,128)(2,1)} async-done(((bf16[32,1,9,1024]{3,0,2,1:T(8,128)(2,1)}), bf16[256,1,9,1024]{3,0,2,1:T(8,128)(2,1)}) %all-gather.11.cloned.1.call-update) | async-done | bytes 4718608 | tf_op jit(solution)/shard_map/all_gather | solution.py:27
  673.6 8.7 copy.26
  682.3 9.9 reshape.500
  692.2 7.0 fusion.14
  700.6 4.4 convert_bitcast_fusion
  707.3 7.0 convolution_bitcast_fusion
  714.3 49.8 %reduce-scatter.5.cloned.1.call-done = bf16[1,1,288,1024]{3,2,1,0:T(8,128)(2,1)} async-done(((bf16[1,8,288,1024]{3,2,1,0:T(8,128)(2,1)}), bf16[1,1,288,1024]{3,2,1,0:T(8,128)(2,1)}) %reduce-scatter.5.cloned.1.call-update) | async-done | bytes 589840 | tf_op jit(solution)/shard_map/reduce_scatter | solution.py:34
  764.1 2.2 reshape.501
  766.3 7.5 all-to-all-start.3
  773.7 7.1 convolution_bitcast_fusion.1
  780.8 8.6 all-to-all-done.3
  789.4 1.4 reshape.502
  790.8 2.0 gather_fusion.1
  792.8 2.3 fusion.37
  796.3 75.8 %all-reduce.2 = (f32[1]{0:T(128)}, f32[1024]{0:T(1024)}) all-reduce(f32[1]{0:T(128)} %bitcast.20, f32[1024]{0:T(1024)S(1)} %get-tuple-element.6), channel_id=1, replica_groups=mesh['dp'=8,'expert'=32] {'dp','expert'}, use_global_device_ids=true, to_apply=%region_13.14 | all-reduce | flops 1025 | bytes 8200 | tf_op jit(solution)/shard_map/psum | solution.py:133
  872.1 142.3 %all-reduce.6.cloned.1.call-done = f32[1024,32]{0,1:T(8,128)} async-done(((f32[1024,32]{0,1:T(8,128)}), f32[1024,32]{0,1:T(8,128)}) %all-reduce.6.cloned.1.call-update) | async-done | bytes 131088 | tf_op jit(solution)/shard_map/psum | solution.py:133
  1014.4 1.6 copy.37
  (117 shorter events, 27.8 us)
Async XLA Ops:
  7.2 111.4 %copy-start = (bf16[1,1024,512]{2,1,0:T(8,128)(2,1)S(1)}, bf16[1,1024,512]{2,1,0:T(8,128)(2,1)}, u32[]{:S(2)}) copy-start(bf16[1,1024,512]{2,1,0:T(8,128)(2,1)} %param.14) | copy-start | bytes 3145732
  7.2 92.8 %all-gather.7.cloned.1.call-start = ((), (), s32[]{:S(2)}) async-start(), calls=%async_computation.9 | async-start | bytes 5308416 | tf_op jit(solution)/shard_map/all_gather | solution.py:27
  8.5 199.2 %copy-start.11 = (f32[212]{0:T(256)}, f32[212]{0:T(256)S(1)}, u32[]{:S(2)}) copy-start(f32[212]{0:T(256)S(1)} %broadcast_multiply_fusion.3) | copy-start | bytes 2548
  9.8 197.9 %copy-start.15 = (f32[212]{0:T(256)}, f32[212]{0:T(256)S(1)}, u32[]{:S(2)}) copy-start(f32[212]{0:T(256)S(1)} %add_rsqrt_fusion) | copy-start | bytes 2548
  12.8 127.0 %copy-start.22 = (s32[212,1]{0,1:T(1,128)}, s32[212,1]{0,1:T(1,128)S(1)}, u32[]{:S(2)}) copy-start(s32[212,1]{0,1:T(1,128)S(1)} %compare_select_fusion) | copy-start | bytes 2548
  39.4 158.6 %reduce-scatter.3.cloned.1.call-start = ((), (), s32[]{:S(2)}) async-start(), calls=%async_computation.6 | async-start | bytes 5308416 | tf_op jit(solution)/shard_map/reduce_scatter | solution.py:34
  118.6 16.3 %copy-start.25 = (bf16[1,512,1024]{2,1,0:T(8,128)(2,1)S(1)}, bf16[1,512,1024]{2,1,0:T(8,128)(2,1)}, u32[]{:S(2)}) copy-start(bf16[1,512,1024]{2,1,0:T(8,128)(2,1)} %param.15) | copy-start | bytes 3145732
  133.4 1.4 copy-start.27
  139.0 68.7 %copy-start.1 = (bf16[1,212,1024]{2,1,0:T(8,128)(2,1)S(1)}, bf16[1,212,1024]{2,1,0:T(8,128)(2,1)}, u32[]{:S(2)}) copy-start(bf16[1,212,1024]{2,1,0:T(8,128)(2,1)} %param.9) | copy-start | bytes 1302532
  139.0 68.7 %copy-start.9 = (f32[1024]{0:T(1024)S(1)}, f32[1024]{0:T(1024)}, u32[]{:S(2)}) copy-start(f32[1024]{0:T(1024)} %param.12) | copy-start | bytes 12292
  139.0 69.0 %copy-start.7 = (f32[1024,32]{0,1:T(8,128)S(1)}, f32[1024,32]{0,1:T(8,128)}, u32[]{:S(2)}) copy-start(f32[1024,32]{0,1:T(8,128)} %param.13) | copy-start | bytes 393220
  139.0 69.0 %copy-start.13 = (s32[1,212,1]{1,2,0:T(1,128)S(1)}, s32[1,212,1]{1,2,0:T(1,128)}, u32[]{:S(2)}) copy-start(s32[1,212,1]{1,2,0:T(1,128)} %param.10) | copy-start | bytes 2548
  139.8 85.0 %copy-start.23 = (f32[16]{0:T(128)}, f32[16]{0:T(128)S(1)}, u32[]{:S(2)}) copy-start(f32[16]{0:T(128)S(1)} %compare_convert_fusion) | copy-start | bytes 196
  139.8 83.7 %copy-start.17 = (s32[1024]{0:T(1024)}, s32[1024]{0:T(1024)S(1)}, u32[]{:S(2)}) copy-start(s32[1024]{0:T(1024)S(1)} %pad_clamp_fusion) | copy-start | bytes 12292
  200.2 23.0 %all-to-all-start.1 = ((bf16[1,32,9,1024]{3,2,0,1:T(8,128)(2,1)}), bf16[1,32,9,1024]{3,2,0,1:T(8,128)(2,1)S(1)}, u32[]{:S(2)}, u32[]{:S(2)}) async-start(bf16[1,32,9,1024]{3,2,0,1:T(8,128)(2,1)} %bitcast.148), calls=%async_computation.2 | async-start | bytes 2097152 | tf_op jit(solution)/shard_map/all_to_all | solution.py:41
  207.7 117.8 %all-gather.9.cloned.1.call-start = ((), (), s32[]{:S(2)}) async-start(), calls=%async_computation.10 | async-start | bytes 1052672 | tf_op jit(solution)/shard_map/all_gather | solution.py:99
  208.8 14.7 %copy-start.18 = (f32[212]{0:T(256)}, f32[212]{0:T(256)S(1)}, u32[]{:S(2)}) copy-start(f32[212]{0:T(256)S(1)} %fusion.16) | copy-start | bytes 2548
  208.8 15.8 %copy-start.20 = (f32[212]{0:T(256)}, f32[212]{0:T(256)S(1)}, u32[]{:S(2)}) copy-start(f32[212]{0:T(256)S(1)} %add_divide_fusion) | copy-start | bytes 2548
  224.6 5.2 copy-start.2
  226.8 359.4 %copy-start.8 = (f32[1024]{0:T(1024)S(1)}, f32[1024]{0:T(1024)}, u32[]{:S(2)}) copy-start(f32[1024]{0:T(1024)} %broadcast_divide_fusion) | copy-start | bytes 12292
  226.8 359.4 %all-reduce.8.cloned.1.call-start = ((), (), s32[]{:S(2)}) async-start(), calls=%async_computation.12 | async-start | bytes 2097152
  228.4 360.6 %copy-start.24 = (f32[16]{0:T(128)S(1)}, f32[16]{0:T(128)}, u32[]{:S(2)}) copy-start(f32[16]{0:T(128)} %copy-done.23) | copy-start | bytes 196
  228.4 360.7 %copy-start.21 = (f32[212]{0:T(256)S(1)}, f32[212]{0:T(256)}, u32[]{:S(2)}) copy-start(f32[212]{0:T(256)} %copy-done.20) | copy-start | bytes 2548
  329.6 344.0 %all-gather.11.cloned.1.call-start = ((), (), s32[]{:S(2)}) async-start(), calls=%async_computation.11 | async-start | bytes 5308416 | tf_op jit(solution)/shard_map/all_gather | solution.py:27
  616.5 147.6 %reduce-scatter.5.cloned.1.call-start = ((), (), s32[]{:S(2)}) async-start(), calls=%async_computation.7 | async-start | bytes 5308416 | tf_op jit(solution)/shard_map/reduce_scatter | solution.py:34
  682.3 9.9 copy-start.26
  699.2 1.4 copy-start.6
  705.1 309.3 %all-reduce.6.cloned.1.call-start = ((), (), s32[]{:S(2)}) async-start(), calls=%async_computation.8 | async-start | bytes 262144 | tf_op jit(solution)/shard_map/psum | solution.py:133
  766.3 23.1 %all-to-all-start.3 = ((bf16[1,32,9,1024]{3,2,0,1:T(8,128)(2,1)}), bf16[1,32,9,1024]{3,2,0,1:T(8,128)(2,1)}, u32[]{:S(2)}, u32[]{:S(2)}) async-start(bf16[1,32,9,1024]{3,2,0,1:T(8,128)(2,1)} %bitcast.30), calls=%async_computation.5 | async-start | bytes 2097152 | tf_op jit(solution)/shard_map/all_to_all | solution.py:41
  780.8 12.0 %copy-start.10 = (f32[1024]{0:T(1024)S(1)}, f32[1024]{0:T(1024)}, u32[]{:S(2)}) copy-start(f32[1024]{0:T(1024)} %param.12) | copy-start | bytes 12292
  780.8 12.0 %copy-start.12 = (f32[212]{0:T(256)S(1)}, f32[212]{0:T(256)}, u32[]{:S(2)}) copy-start(f32[212]{0:T(256)} %copy-done.11) | copy-start | bytes 2548
  780.8 12.0 %copy-start.16 = (f32[212]{0:T(256)S(1)}, f32[212]{0:T(256)}, u32[]{:S(2)}) copy-start(f32[212]{0:T(256)} %copy-done.15) | copy-start | bytes 2548
  (5 other events, 5.5 us)
Sparse Core Ops, SparseCore 0:
  39.6 60.3 all-gather.6
  139.2 58.8 reduce-scatter.2
  226.9 98.4 all-gather.8
  331.3 254.8 all-reduce.7
  616.6 56.8 all-gather.10
  705.2 58.8 reduce-scatter.4
  771.1 243.2 all-reduce.5
where the time goes:
time: 1020 us
  waiting for transfers between devices  741 us (73%)
  blocking collectives  121 us (12%)
  local copies, waits for them, and re-layouts  56.6 us (6%)
  matrix products  49.8 us (5%)
  between operations  19.9 us (2%)
  other arithmetic  18.6 us (2%)
  starting transfers between devices  15.8 us (2%)
    unnamed x8, waiting for transfers between devices  255 us
    psum x1, waiting for transfers between devices, body(): lax.psum((loss_term, router_part, gain_partial_term), ('dp', 'expert'))  142 us
    all_gather x2, waiting for transfers between devices, deliver(): whole = lax.all_gather(shaped, 'dp', axis=1, tiled=True)  117 us
    reduce_scatter x2, waiting for transfers between devices, give_back(): lax.psum_scatter(partial_value.reshape(local, n_dp, n_expert * slots, wid...  108 us
    all_gather x1, waiting for transfers between devices, body(): v_all = lax.all_gather(v, ('dp', 'expert'), axis=0, tiled=True)  95.7 us
    psum x1, blocking collectives, body(): lax.psum((loss_term, router_part, gain_partial_term), ('dp', 'expert'))  75.8 us
    all_to_all x2, blocking collectives, deliver(): lax.all_to_all(buffer.reshape(experts, 1, slots, width), 'expert', split_...  45.2 us
    all_to_all x2, waiting for transfers between devices, give_back(): lax.all_to_all(rounded, 'expert', split_axis=1, concat_axis=0, tiled=True)  23 us
  transfers between devices with their start and end apart: 9, of which 9 were waited for; matrix products, arithmetic and copies ran while one was open for 3% of the time, Pallas kernels for 0%

commit v1 on v0

--- a/solution.py
+++ b/solution.py
@@ -131,7 +131,7 @@
     ) * inverse_deviation
     grad_tokens = (dy + normed_input_gradient).astype(jnp.bfloat16).reshape(pair_dev, SEQ, D)
     loss, grad_router, layer_gain_gradient = lax.psum(
-        (loss_term, router_part, gain_partial_term), ("dp", "expert")
+        lax.psum((loss_term, router_part, gain_partial_term), "dp"), "expert"
     )
     return (loss.reshape(1), grad_tokens, grad_up, grad_down, grad_router, layer_gain_gradient)
 

time: 1020 us -> 933 us (0.915)
  waiting for transfers between devices: 741 us -> 645 us
    psum x1 -> x2, waiting for transfers between devices: 142 us -> 45.4 us  [the longest x1 41.2 us: body(): lax.psum((loss_term, router_part, gain_partial_term), 'dp')]
    psum x1 -> x2, blocking collectives: 75.8 us -> 76.6 us  [the longest x1 60.3 us: body(): lax.psum(lax.psum((loss_term, router_part, gain_partial_term), 'dp'), 'ex...]
    unnamed x8 -> x9, waiting for transfers between devices: 255 us -> 255 us
  transfers between devices with their start and end apart: 9 -> 10, of which waited for: 9 -> 10; matrix products, arithmetic and copies ran while one was open for 3% -> 6% of each run, Pallas kernels for 0% -> 0%
where the time goes in v1:
time: 933 us; the launch traced here: 930 us
  waiting for transfers between devices  645 us (69%)
  blocking collectives  122 us (13%)
  local copies, waits for them, and re-layouts  56.5 us (6%)
  matrix products  50.7 us (5%)
  other arithmetic  20.2 us (2%)
  between operations  19.8 us (2%)
  starting transfers between devices  15.9 us (2%)
    unnamed x9, waiting for transfers between devices  255 us
    all_gather x2, waiting for transfers between devices, deliver(): whole = lax.all_gather(shaped, 'dp', axis=1, tiled=True)  113 us
    reduce_scatter x2, waiting for transfers between devices, give_back(): lax.psum_scatter(partial_value.reshape(local, n_dp, n_expert * slots, wid...  113 us
    all_gather x1, waiting for transfers between devices, body(): v_all = lax.all_gather(v, ('dp', 'expert'), axis=0, tiled=True)  95.7 us
    psum x1, blocking collectives, body(): lax.psum(lax.psum((loss_term, router_part, gain_partial_term), 'dp'), 'ex...  60.3 us
    all_to_all x2, blocking collectives, deliver(): lax.all_to_all(buffer.reshape(experts, 1, slots, width), 'expert', split_...  45.2 us
    psum x1, waiting for transfers between devices, body(): lax.psum((loss_term, router_part, gain_partial_term), 'dp')  41.2 us
    all_to_all x2, waiting for transfers between devices, give_back(): lax.all_to_all(rounded, 'expert', split_axis=1, concat_axis=0, tiled=True)  23.1 us
  transfers between devices with their start and end apart: 10, of which 10 were waited for; matrix products, arithmetic and copies ran while one was open for 6% of the time, Pallas kernels for 0%

profile of v1, /device:TPU:8, one launch (start us, length us, event | category | flops | bytes accessed | tf_op | source)
XLA Modules:
  0.0 929.7 jit_solution(6629440776206208300)
XLA Ops:
  12.8 2.3 scatter_custom_fusion
  15.4 22.9 %all_to_all.16 = bf16[32,1,9,1024]{3,2,1,0:T(8,128)(2,1)S(1)} all-to-all(bf16[32,1,9,1024]{3,2,1,0:T(8,128)(2,1)S(1)} %bitcast.149), channel_id=1, replica_groups=mesh['dp'=8,'expert'=32] {'expert'}, dimensions={0} | all-to-all | bytes 1179648 | tf_op jit(solution)/shard_map/all_to_all | solution.py:23
  39.7 60.3 %all-gather.7.cloned.1.call-done = bf16[256,1,9,1024]{3,0,2,1:T(8,128)(2,1)} async-done(((bf16[32,1,9,1024]{3,0,2,1:T(8,128)(2,1)}), bf16[256,1,9,1024]{3,0,2,1:T(8,128)(2,1)}) %all-gather.7.cloned.1.call-update) | async-done | bytes 4718608 | tf_op jit(solution)/shard_map/all_gather | solution.py:27
  100.0 8.7 copy.22
  108.7 9.8 %reshape.491 = bf16[2304,1024]{1,0:T(8,128)(2,1)} reshape(bf16[256,1,9,1024]{3,2,0,1:T(8,128)(2,1)} %copy.22) | data formatting | bytes 9437184 | tf_op jit(solution)/shard_map/reshape.7
  118.6 14.9 %fusion.2 = (bf16[2304,512]{1,0:T(8,128)(2,1)S(1)}, f32[2304,512]{1,0:T(8,128)}) fusion(bf16[2304,1024]{1,0:T(8,128)(2,1)} %reshape.491, bf16[1,1024,512]{2,1,0:T(8,128)(2,1)S(1)} %copy-done), kind=kOutput, calls=%fused_computation.9 | convolution fusion | flops 2492596224 | bytes 12845056 | tf_op jit(solution)/shard_map/erd,edf->erf/dot_general | solution.py:76
  134.8 4.2 convert_bitcast_fusion.1
  139.8 58.3 %reduce-scatter.3.cloned.1.call-done = bf16[1,1,288,1024]{3,2,1,0:T(8,128)(2,1)} async-done(((bf16[1,8,288,1024]{3,2,1,0:T(8,128)(2,1)}), bf16[1,1,288,1024]{3,2,1,0:T(8,128)(2,1)}) %reduce-scatter.3.cloned.1.call-update) | async-done | bytes 589840 | tf_op jit(solution)/shard_map/reduce_scatter | solution.py:34
  198.1 2.2 reshape.494
  200.2 7.4 all-to-all-start.1
  208.8 14.4 %all-to-all-done.1 = bf16[1,32,9,1024]{3,2,0,1:T(8,128)(2,1)S(1)} async-done(((bf16[1,32,9,1024]{3,2,0,1:T(8,128)(2,1)}), bf16[1,32,9,1024]{3,2,0,1:T(8,128)(2,1)S(1)}, u32[]{:S(2)}, u32[]{:S(2)}) %all-to-all-start.1) | async-done | bytes 589856 | tf_op jit(solution)/shard_map/all_to_all | solution.py:41
  229.8 95.7 %all-gather.9.cloned.1.call-done = f32[262144]{0:T(1024)} async-done(((f32[1024]{0:T(1024)}), f32[262144]{0:T(1024)}) %all-gather.9.cloned.1.call-update) | async-done | bytes 1048592 | tf_op jit(solution)/shard_map/all_gather | solution.py:99
  331.5 254.7 %all-reduce.12.cloned.1.call-done = f32[256,1024]{1,0:T(8,128)} async-done(((f32[256,1024]{1,0:T(8,128)}), f32[256,1024]{1,0:T(8,128)}) %all-reduce.12.cloned.1.call-update) | async-done | bytes 1048592
  589.2 2.5 scatter_custom_fusion.1
  593.0 22.3 %all_to_all.17 = bf16[32,1,9,1024]{3,2,1,0:T(8,128)(2,1)S(1)} all-to-all(bf16[32,1,9,1024]{3,2,1,0:T(8,128)(2,1)S(1)} %bitcast.150), channel_id=1, replica_groups=mesh['dp'=8,'expert'=32] {'expert'}, dimensions={0} | all-to-all | bytes 1179648 | tf_op jit(solution)/shard_map/all_to_all | solution.py:23
  618.5 2.0 fusion.51
  620.5 53.0 %all-gather.11.cloned.1.call-done = bf16[256,1,9,1024]{3,0,2,1:T(8,128)(2,1)} async-done(((bf16[32,1,9,1024]{3,0,2,1:T(8,128)(2,1)}), bf16[256,1,9,1024]{3,0,2,1:T(8,128)(2,1)}) %all-gather.11.cloned.1.call-update) | async-done | bytes 4718608 | tf_op jit(solution)/shard_map/all_gather | solution.py:27
  673.6 8.7 copy.26
  682.3 9.9 %reshape.500 = bf16[2304,1024]{1,0:T(8,128)(2,1)} reshape(bf16[256,1,9,1024]{3,2,0,1:T(8,128)(2,1)} %copy.26) | data formatting | bytes 9437184 | tf_op jit(solution)/shard_map/reshape.64
  692.2 6.8 fusion.14
  700.4 4.4 convert_bitcast_fusion
  705.7 41.2 %all-reduce.8.cloned.1.call-done = f32[1024,32]{0,1:T(8,128)} async-done(((f32[1024,32]{0,1:T(8,128)}), f32[1024,32]{0,1:T(8,128)}) %all-reduce.8.cloned.1.call-update) | async-done | bytes 131088 | tf_op jit(solution)/shard_map/psum | solution.py:134
  747.0 7.0 convolution_bitcast_fusion
  753.9 54.3 %reduce-scatter.5.cloned.1.call-done = bf16[1,1,288,1024]{3,2,1,0:T(8,128)(2,1)} async-done(((bf16[1,8,288,1024]{3,2,1,0:T(8,128)(2,1)}), bf16[1,1,288,1024]{3,2,1,0:T(8,128)(2,1)}) %reduce-scatter.5.cloned.1.call-update) | async-done | bytes 589840 | tf_op jit(solution)/shard_map/reduce_scatter | solution.py:34
  808.2 2.2 reshape.501
  810.4 7.5 all-to-all-start.3
  817.9 7.1 convolution_bitcast_fusion.1
  824.9 8.6 all-to-all-done.3
  837.0 2.3 fusion.37
  840.5 16.2 %all-reduce.3 = (f32[]{:T(128)}, f32[1024]{0:T(1024)S(1)}) all-reduce(f32[]{:T(128)S(6)} %div.153, f32[1024]{0:T(1024)S(1)} %get-tuple-element.6), channel_id=1, replica_groups=mesh['dp'=8,'expert'=32] {'dp'}, use_global_device_ids=true, to_apply=%region_13.14 | all-reduce | flops 1025 | bytes 8200 | tf_op jit(solution)/shard_map/psum | solution.py:134
  856.7 60.3 %all-reduce.2 = (f32[1]{0:T(128)}, f32[1024]{0:T(1024)}) all-reduce(f32[1]{0:T(128)} %bitcast.20, f32[1024]{0:T(1024)S(1)} %get-tuple-element.12), channel_id=1, replica_groups=mesh['dp'=8,'expert'=32] {'expert'}, use_global_device_ids=true, to_apply=%region_14.15 | all-reduce | flops 1025 | bytes 8200 | tf_op jit(solution)/shard_map/psum | solution.py:133
  917.1 4.3 all-reduce.10.cloned.1.call-done
  (113 shorter events, 33.5 us)
Async XLA Ops:
  7.2 111.4 %copy-start = (bf16[1,1024,512]{2,1,0:T(8,128)(2,1)S(1)}, bf16[1,1024,512]{2,1,0:T(8,128)(2,1)}, u32[]{:S(2)}) copy-start(bf16[1,1024,512]{2,1,0:T(8,128)(2,1)} %param.14) | copy-start | bytes 3145732
  7.2 92.8 %all-gather.7.cloned.1.call-start = ((), (), s32[]{:S(2)}) async-start(), calls=%async_computation.10 | async-start | bytes 5308416 | tf_op jit(solution)/shard_map/all_gather | solution.py:27
  8.5 199.2 %copy-start.9 = (f32[212]{0:T(256)}, f32[212]{0:T(256)S(1)}, u32[]{:S(2)}) copy-start(f32[212]{0:T(256)S(1)} %broadcast_multiply_fusion.3) | copy-start | bytes 2548
  9.8 197.9 %copy-start.13 = (f32[212]{0:T(256)}, f32[212]{0:T(256)S(1)}, u32[]{:S(2)}) copy-start(f32[212]{0:T(256)S(1)} %add_rsqrt_fusion) | copy-start | bytes 2548
  12.8 127.0 %copy-start.19 = (s32[212,1]{0,1:T(1,128)}, s32[212,1]{0,1:T(1,128)S(1)}, u32[]{:S(2)}) copy-start(s32[212,1]{0,1:T(1,128)S(1)} %compare_select_fusion) | copy-start | bytes 2548
  39.4 158.6 %reduce-scatter.3.cloned.1.call-start = ((), (), s32[]{:S(2)}) async-start(), calls=%async_computation.6 | async-start | bytes 5308416 | tf_op jit(solution)/shard_map/reduce_scatter | solution.py:34
  118.6 16.3 %copy-start.22 = (bf16[1,512,1024]{2,1,0:T(8,128)(2,1)S(1)}, bf16[1,512,1024]{2,1,0:T(8,128)(2,1)}, u32[]{:S(2)}) copy-start(bf16[1,512,1024]{2,1,0:T(8,128)(2,1)} %param.15) | copy-start | bytes 3145732
  139.0 68.7 %copy-start.1 = (bf16[1,212,1024]{2,1,0:T(8,128)(2,1)S(1)}, bf16[1,212,1024]{2,1,0:T(8,128)(2,1)}, u32[]{:S(2)}) copy-start(bf16[1,212,1024]{2,1,0:T(8,128)(2,1)} %param.9) | copy-start | bytes 1302532
  139.0 68.7 %copy-start.7 = (f32[1024]{0:T(1024)S(1)}, f32[1024]{0:T(1024)}, u32[]{:S(2)}) copy-start(f32[1024]{0:T(1024)} %param.12) | copy-start | bytes 12292
  139.0 69.0 %copy-start.5 = (f32[1024,32]{0,1:T(8,128)S(1)}, f32[1024,32]{0,1:T(8,128)}, u32[]{:S(2)}) copy-start(f32[1024,32]{0,1:T(8,128)} %param.13) | copy-start | bytes 393220
  139.0 69.0 %copy-start.11 = (s32[1,212,1]{1,2,0:T(1,128)S(1)}, s32[1,212,1]{1,2,0:T(1,128)}, u32[]{:S(2)}) copy-start(s32[1,212,1]{1,2,0:T(1,128)} %param.10) | copy-start | bytes 2548
  139.8 85.0 %copy-start.20 = (f32[16]{0:T(128)}, f32[16]{0:T(128)S(1)}, u32[]{:S(2)}) copy-start(f32[16]{0:T(128)S(1)} %compare_convert_fusion) | copy-start | bytes 196
  139.8 83.7 %copy-start.15 = (s32[1024]{0:T(1024)}, s32[1024]{0:T(1024)S(1)}, u32[]{:S(2)}) copy-start(s32[1024]{0:T(1024)S(1)} %pad_clamp_fusion) | copy-start | bytes 12292
  200.2 23.0 %all-to-all-start.1 = ((bf16[1,32,9,1024]{3,2,0,1:T(8,128)(2,1)}), bf16[1,32,9,1024]{3,2,0,1:T(8,128)(2,1)S(1)}, u32[]{:S(2)}, u32[]{:S(2)}) async-start(bf16[1,32,9,1024]{3,2,0,1:T(8,128)(2,1)} %bitcast.148), calls=%async_computation.2 | async-start | bytes 2097152 | tf_op jit(solution)/shard_map/all_to_all | solution.py:41
  207.7 117.8 %all-gather.9.cloned.1.call-start = ((), (), s32[]{:S(2)}) async-start(), calls=%async_computation.11 | async-start | bytes 1052672 | tf_op jit(solution)/shard_map/all_gather | solution.py:99
  208.8 14.7 %copy-start.16 = (f32[212]{0:T(256)}, f32[212]{0:T(256)S(1)}, u32[]{:S(2)}) copy-start(f32[212]{0:T(256)S(1)} %fusion.16) | copy-start | bytes 2548
  208.8 15.8 %copy-start.17 = (f32[212]{0:T(256)}, f32[212]{0:T(256)S(1)}, u32[]{:S(2)}) copy-start(f32[212]{0:T(256)S(1)} %add_divide_fusion) | copy-start | bytes 2548
  224.6 5.2 copy-start.2
  226.8 359.4 %copy-start.6 = (f32[1024]{0:T(1024)S(1)}, f32[1024]{0:T(1024)}, u32[]{:S(2)}) copy-start(f32[1024]{0:T(1024)} %broadcast_divide_fusion) | copy-start | bytes 12292
  226.8 359.4 %all-reduce.12.cloned.1.call-start = ((), (), s32[]{:S(2)}) async-start(), calls=%async_computation.13 | async-start | bytes 2097152
  228.4 360.6 %copy-start.21 = (f32[16]{0:T(128)S(1)}, f32[16]{0:T(128)}, u32[]{:S(2)}) copy-start(f32[16]{0:T(128)} %copy-done.20) | copy-start | bytes 196
  228.4 360.7 %copy-start.18 = (f32[212]{0:T(256)S(1)}, f32[212]{0:T(256)}, u32[]{:S(2)}) copy-start(f32[212]{0:T(256)} %copy-done.17) | copy-start | bytes 2548
  329.6 344.0 %all-gather.11.cloned.1.call-start = ((), (), s32[]{:S(2)}) async-start(), calls=%async_computation.12 | async-start | bytes 5308416 | tf_op jit(solution)/shard_map/all_gather | solution.py:27
  616.5 130.4 %all-reduce.8.cloned.1.call-start = ((), (), s32[]{:S(2)}) async-start(), calls=%async_computation.8 | async-start | bytes 262144 | tf_op jit(solution)/shard_map/psum | solution.py:134
  620.5 187.8 %reduce-scatter.5.cloned.1.call-start = ((), (), s32[]{:S(2)}) async-start(), calls=%async_computation.7 | async-start | bytes 5308416 | tf_op jit(solution)/shard_map/reduce_scatter | solution.py:34
  699.0 1.4 copy-start.4
  704.8 216.5 %all-reduce.10.cloned.1.call-start = ((), (), s32[]{:S(2)}) async-start(), calls=%async_computation.9 | async-start | bytes 262144 | tf_op jit(solution)/shard_map/psum | solution.py:133
  810.4 23.2 %all-to-all-start.3 = ((bf16[1,32,9,1024]{3,2,0,1:T(8,128)(2,1)}), bf16[1,32,9,1024]{3,2,0,1:T(8,128)(2,1)}, u32[]{:S(2)}, u32[]{:S(2)}) async-start(bf16[1,32,9,1024]{3,2,0,1:T(8,128)(2,1)} %bitcast.30), calls=%async_computation.5 | async-start | bytes 2097152 | tf_op jit(solution)/shard_map/all_to_all | solution.py:41
  824.9 12.1 %copy-start.8 = (f32[1024]{0:T(1024)S(1)}, f32[1024]{0:T(1024)}, u32[]{:S(2)}) copy-start(f32[1024]{0:T(1024)} %param.12) | copy-start | bytes 12292
  824.9 12.1 %copy-start.10 = (f32[212]{0:T(256)S(1)}, f32[212]{0:T(256)}, u32[]{:S(2)}) copy-start(f32[212]{0:T(256)} %copy-done.9) | copy-start | bytes 2548
  824.9 12.1 %copy-start.12 = (s32[1,212,1]{1,2,0:T(1,128)S(1)}, s32[1,212,1]{1,2,0:T(1,128)}, u32[]{:S(2)}) copy-start(s32[1,212,1]{1,2,0:T(1,128)} %param.10) | copy-start | bytes 2548
  824.9 12.1 %copy-start.14 = (f32[212]{0:T(256)S(1)}, f32[212]{0:T(256)}, u32[]{:S(2)}) copy-start(f32[212]{0:T(256)} %copy-done.13) | copy-start | bytes 2548
  (2 other events, 2.2 us)
Sparse Core Ops, SparseCore 0:
  39.6 60.3 all-gather.6
  139.2 58.8 reduce-scatter.2
  226.9 98.4 all-gather.8
  331.3 254.8 all-reduce.11
  616.7 56.8 all-gather.10
  676.4 70.4 all-reduce.7
  749.5 58.7 reduce-scatter.4
  811.5 109.8 all-reduce.9
